TPU v7x, 768 devices: a whole 4x8x12 slice. The times are simulated.
768 devices in a mesh: replica: 192 (over z_hi, y, x, core), fsdp: 4 (over z_lo).
Axes of the slice: x: 4, y: 8, z: 12 (z_hi: 3, z_lo: 4; z = z_hi * 4 + z_lo), core: 2. Of those that a mesh axis runs over, the one named last changes fastest.
Arguments:
- activations: bfloat16 [196608, 4096], P(('replica', 'fsdp')), may hold values from -6 to 6
- output_grads: bfloat16 [196608, 512], P(('replica', 'fsdp')), may hold values from -0.1875 to 0.1875
- momentum: bfloat16 [192, 4096, 512], P('replica', 'fsdp'), may hold values from -6 to 6
- chosen_blocks: int32 [192, 64, 8], P('replica', 'fsdp'), may hold values from 0 to 255, as said below
Outputs:
- momentum_next: bfloat16 [192, 4096, 512], P('replica', 'fsdp')
- update: float32 [4096, 512], P('fsdp')
Inputs may be any that keep to these rules, and one draw needn't show every extreme that they name: `chosen_blocks`: the 8 numbers of each span row of each replica are different block numbers.
All inputs are finite; a program needn't handle non-finite values.
Results may differ from a plain program's by a relative error of at most 0.013.
Values may be sent and summed in bfloat16 or wider, within the bound.
A program may use at most 64 MiB of HBM per device.

v0:
```python
import jax
import jax.numpy as jnp
from jax import lax
from jax.sharding import PartitionSpec as P


def cosine_table(size):
    order = lax.broadcasted_iota(jnp.float32, (size, size), 0)
    place = lax.broadcasted_iota(jnp.float32, (size, size), 1)
    factor = jnp.where(
        order == 0.0, jnp.sqrt(jnp.float32(1.0 / size)), jnp.sqrt(jnp.float32(2.0 / size))
    )
    return factor * jnp.cos(jnp.float32(jnp.pi) * (2.0 * place + 1.0) * order / (2.0 * size))


def forward_blocks(field, table, size, block_len):
    rows = field.shape[0] // size
    cols = field.shape[1] // size
    shaped = field.reshape(rows, size, cols, size)
    coeffs = jnp.einsum("pu,cujv,qv->cjpq", table, shaped, table, precision=lax.Precision.HIGHEST)
    return coeffs.reshape(rows, cols * (size * size // block_len), block_len)


def inverse_blocks(coeffs, table, size, block_len):
    rows = coeffs.shape[0]
    cols = coeffs.shape[1] * block_len // (size * size)
    shaped = coeffs.reshape(rows, cols, size, size)
    field = jnp.einsum("pu,cjpq,qv->cujv", table, shaped, table, precision=lax.Precision.HIGHEST)
    return field.reshape(rows * size, cols * size)


def body(activations, output_grads, momentum, chosen_blocks):
    size = 64
    block_len = 128
    width_out = momentum.shape[2]
    nblocks = width_out // size * (size * size // block_len)
    table = cosine_table(size)
    grad = lax.psum_scatter(
        lax.dot_general(
            activations, output_grads, (((0,), (0,)), ((), ())), preferred_element_type=jnp.float32
        ).astype(jnp.bfloat16),
        "fsdp",
        scatter_dimension=0,
        tiled=True,
    ).astype(jnp.float32)
    moment = 0.9 * momentum[0].astype(jnp.float32) + grad
    coeffs = forward_blocks(moment, table, size, block_len)
    picks = chosen_blocks[0]
    numbers = lax.broadcasted_iota(jnp.int32, (1, 1, nblocks), 2)
    selector = (picks[:, :, None] == numbers).astype(jnp.float32)
    mask = jnp.sum(selector, axis=1)
    kept = coeffs * (1.0 - mask[:, :, None])
    moment_next = inverse_blocks(kept, table, size, block_len).astype(jnp.bfloat16)
    values = jnp.einsum("ckb,cbv->ckv", selector, coeffs, precision=lax.Precision.HIGHEST).astype(
        jnp.bfloat16
    )
    piece_values = lax.all_gather(values[None], "replica", axis=0, tiled=True)
    piece_numbers = lax.all_gather(picks[None], "replica", axis=0, tiled=True)
    onehot = (piece_numbers[:, :, :, None] == numbers[None]).astype(jnp.bfloat16)
    total = jnp.einsum("rckb,rckv->cbv", onehot, piece_values, preferred_element_type=jnp.float32)
    update = inverse_blocks(total, table, size, block_len)
    return (moment_next[None], update)


def solution(mesh):
    return jax.shard_map(
        body,
        mesh=mesh,
        in_specs=(
            P(("replica", "fsdp"), None),
            P(("replica", "fsdp"), None),
            P("replica", "fsdp", None),
            P("replica", "fsdp", None),
        ),
        out_specs=(P("replica", "fsdp", None), P("fsdp", None)),
        check_vma=False,
    )
```

profile of v0, /device:TPU:1, one launch (start us, length us, event | category | flops | bytes accessed | tf_op | source)
XLA Modules:
  0.0 538.2 jit_solution(11507531804551297121)
XLA Ops:
  7.2 0.0 copy-start
  7.2 0.0 reduce-scatter.2.cloned.1.call-start
  7.2 1.5 copy-done
  8.8 4.2 convolution_convert_fusion
  12.9 0.0 copy-start.2
  12.9 0.0 copy-start.1
  12.9 0.0 reduce-scatter.2.cloned.1.call-update
  13.0 0.0 all-gather.3.cloned.1.call-start
  13.0 0.6 copy-done.2
  13.6 0.1 copy.29
  13.7 94.4 %reduce-scatter.2.cloned.1.call-done = bf16[1024,512]{1,0:T(8,128)(2,1)} async-done(((bf16[4096,512]{1,0:T(8,128)(2,1)}), bf16[1024,512]{1,0:T(8,128)(2,1)}) %reduce-scatter.2.cloned.1.call-update) | async-done | bytes 1048592 | tf_op jit(solution)/shard_map/reduce_scatter | solution.py:38
  108.1 0.0 copy-done.1
  108.1 2.8 bitcast_add_fusion
  111.0 4.4 reshape.39
  115.4 6.9 %fusion.3 = f32[16,8,64,64]{2,3,1,0:T(8,128)S(1)} fusion(f32[16,64,8,64]{3,2,1,0:T(8,128)} %reshape.39, f32[64]{0:T(128)S(1)} %get-tuple-element.3, f32[64]{0:T(128)S(1)} %multiply_add_fusion, f32[64]{0:T(128)S(1)} %get-tuple-element.2), kind=kOutput, calls=%fused_computation.5 | convolution fusion | flops 402665472 | bytes 4195072 | tf_op jit(solution)/shard_map/pu,cujv,qv->cjpq/dot_general | solution.py:20
  122.3 5.4 fusion.17
  127.6 4.6 reshape.40
  132.3 3.0 convolution_convert_fusion.1
  135.2 0.0 all-gather.3.cloned.1.call-update
  135.3 0.1 convert_reduce_fusion
  135.4 0.1 copy.30
  135.5 0.1 mul.103
  135.6 0.1 copy.31
  135.7 339.8 %all_gather.6 = s32[192,16,8]{1,2,0:T(8,128)S(1)} all-gather(s32[1,16,8]{1,2,0:T(8,128)S(1)} %copy-done.2), channel_id=1, replica_groups=mesh['replica'=192,'fsdp'=4] {'replica'}, dimensions={0}, use_global_device_ids=true | all-gather | bytes 98816 | tf_op jit(solution)/shard_map/all_gather | solution.py:58
  475.5 0.4 copy.35
  475.8 6.7 %fusion.5 = f32[16,8,64,64]{2,3,1,0:T(8,128)S(1)} fusion(f32[16,8,64,64]{3,2,1,0:T(8,128)} %fusion.17, f32[16,8,64]{2,1,0:T(8,128)S(1)} %copy.31, f32[64]{0:T(128)S(1)} %get-tuple-element.3, f32[64]{0:T(128)S(1)} %multiply_add_fusion, f32[64]{0:T(128)S(1)} %get-tuple-element.2), kind=kOutput, calls=%fused_computation.7 | convolution fusion | flops 403189760 | bytes 4227840 | tf_op jit(solution)/shard_map/pu,cjpq,qv->cujv/dot_general | solution.py:28
  482.5 4.0 convert_bitcast_fusion
  486.5 3.1 copy.34
  489.6 4.0 convert_element_type.39
  493.7 0.0 all-gather.3.cloned.1.call-done
  493.7 13.6 %fusion.8 = f32[16,256,128]{2,1,0:T(8,128)} fusion(bf16[192,16,8,128]{3,2,1,0:T(8,128)(2,1)} %bitcast.42, s32[192,16,8]{0,2,1:T(8,128)S(1)} %copy.35), kind=kOutput, calls=%fused_computation.13 | convolution fusion | flops 1616904192 | bytes 8486912 | tf_op jit(solution)/shard_map/rckb,rckv->cbv/dot_general | solution.py:60
  507.3 4.3 reshape.41
  511.6 6.1 %fusion.13 = f32[16,8,64,64]{2,3,1,0:T(8,128)S(1)} fusion(f32[16,8,64,64]{3,2,1,0:T(8,128)} %reshape.41, f32[64]{0:T(128)S(1)} %get-tuple-element.3, f32[64]{0:T(128)S(1)} %multiply_add_fusion, f32[64]{0:T(128)S(1)} %get-tuple-element.2), kind=kOutput, calls=%fused_computation.19 | convolution fusion | flops 402665472 | bytes 4195072 | tf_op jit(solution)/shard_map/pu,cjpq,qv->cujv/dot_general | solution.py:28
  517.7 3.6 convolution_bitcast_fusion
  521.3 5.2 copy.39
  526.6 4.8 reshape.42
  (3 shorter events, 0.0 us)
Async XLA Ops:
  7.2 1.6 copy-start
  7.2 101.0 %reduce-scatter.2.cloned.1.call-start = ((), (), s32[]{:S(2)}) async-start(), calls=%async_computation.1 | async-start | bytes 5242880 | tf_op jit(solution)/shard_map/reduce_scatter | solution.py:38
  12.9 0.7 copy-start.2
  12.9 95.2 %copy-start.1 = (bf16[1,1024,512]{2,1,0:T(8,128)(2,1)S(1)}, bf16[1,1024,512]{2,1,0:T(8,128)(2,1)}, u32[]{:S(2)}) copy-start(bf16[1,1024,512]{2,1,0:T(8,128)(2,1)} %param.6) | copy-start | bytes 3145732
  13.0 480.7 %all-gather.3.cloned.1.call-start = ((), (), s32[]{:S(2)}) async-start(), calls=%async_computation.2 | async-start | bytes 6324224 | tf_op jit(solution)/shard_map/all_gather | solution.py:57
Sparse Core Ops, SparseCore 0:
  13.1 95.0 reduce-scatter.1
  135.4 168.6 all-gather.2
where the time goes:
time: 542 us; the launch traced here: 538 us
  blocking collectives  340 us (63%)
  waiting for transfers between devices  94.5 us (17%)
  matrix products  53.4 us (10%)
  local copies, waits for them, and re-layouts  33.4 us (6%)
  between operations  14.1 us (3%)
    all_gather x1, blocking collectives, body(): piece_numbers = lax.all_gather(picks[None], 'replica', axis=0, tiled=True)  340 us
    reduce_scatter x1, waiting for transfers between devices, body(): lax.psum_scatter(lax.dot_general(activations, output_grads, (((0,), (0,))...  94.4 us
    dot_general x4, matrix products, inverse_blocks(): jnp.einsum('pu,cjpq,qv->cujv', table, shaped, table, precision=lax.Precis...  20.4 us
    dot_general x1, matrix products, body(): jnp.einsum('rckb,rckv->cbv', onehot, piece_values, preferred_element_type...  13.6 us
    dot_general x2, matrix products, forward_blocks(): jnp.einsum('pu,cujv,qv->cjpq', table, shaped, table, precision=lax.Precis...  12.3 us
  transfers between devices with their start and end apart: 2, of which 1 were waited for; matrix products, arithmetic and copies ran while one was open for 3% of the time, Pallas kernels for 0%

commit v1 on v0

v1 whole, which is shorter than its diff:
```python
import math

import jax
import jax.numpy as jnp
import numpy as np
from jax import lax
from jax.experimental import pallas as pl
from jax.experimental.pallas import tpu as pltpu
from jax.sharding import PartitionSpec as P

MESH = pl.DeviceIdType.MESH
F32 = jnp.float32
BF = jnp.bfloat16
SPAN = 64
NX, NY, NZ, NF = 8, 8, 3, 4
SLABS = 4


def tables():
    order = np.arange(SPAN)[:, None]
    place = np.arange(SPAN)[None, :]
    factor = np.where(order == 0, math.sqrt(1.0 / SPAN), math.sqrt(2.0 / SPAN))
    table = factor * np.cos(np.pi * (2 * place + 1) * order / (2 * SPAN))
    block = np.kron(np.eye(4), table).astype(np.float32)
    high = block.astype(jnp.bfloat16)
    low = (block - high.astype(np.float32)).astype(jnp.bfloat16)
    return high, low


def dot(a, b, ca=1, cb=0):
    return lax.dot_general(a, b, (((ca,), (cb,)), ((), ())), preferred_element_type=F32)


def split(a):
    high = a.astype(BF)
    return high, (a - high.astype(F32)).astype(BF)


def dot3(a, b, ca=1, cb=0):
    return dot(a[0], b[0], ca, cb) + dot(a[0], b[1], ca, cb) + dot(a[1], b[0], ca, cb)


def lanes_transform(value, table, cb):
    high, low = split(value)
    width = value.shape[1] // 256
    return jnp.concatenate(
        [
            dot3((high[:, 256 * t : 256 * t + 256], low[:, 256 * t : 256 * t + 256]), table, 1, cb)
            for t in range(width)
        ],
        axis=1,
    )


def iota(shape, dim):
    return lax.broadcasted_iota(jnp.int32, shape, dim)


def fold(value, span_col):
    lane = iota((value.shape[0], 128), 1)
    half = jnp.floor(span_col * 0.5)
    odd = span_col - 2.0 * half
    kept = jnp.zeros((value.shape[0], 128), F32)
    for s in range(4):
        kept = kept + jnp.where(half == float(s), value[:, 128 * s : 128 * s + 128], 0.0)
    kept = jnp.where((lane >> 6).astype(F32) == odd, kept, 0.0)
    return kept + pltpu.roll(kept, 64, 1)


def pack(rows):
    lane = iota((128, 128), 1)
    return jnp.where(lane < 64, rows[:128], rows[128:])


def kernel(
    x_hbm, g_hbm, mom_hbm, pk_ref, ch_ref, cl_ref, cth_ref, ctl_ref,
    out_m, out_u,
    xv, gv, mv, xr, gr, pk_all, csh, csl, jrow, trow, upart, usend, urecv,
    sent, a2, dp, by, zb, fin, mout,
    lsem, pk_s, pk_r, x_s, x_r, g_s, g_r, u_s, u_r, a_s, a_r, b_s, b_r,
    z_s, z_r, y_s, y_r, w_s, w_r, c_s, c_r,
):
    rep = lax.axis_index("replica")
    f = lax.axis_index("fsdp")
    m = lax.rem(rep, NX)
    row = rep - m
    y = lax.rem(lax.div(rep, NX), NY)
    zh = lax.div(rep, NX * NY)
    plane = lax.rem(rep, NX * NY)

    def line_peer(o):
        return (rep, lax.rem(f + o, NF))

    def row_peer(o):
        return (row + lax.rem(m + o, NX), f)

    def col_peer(o):
        return (zh * (NX * NY) + lax.rem(y + o, NY) * NX + m, f)

    def hi_peer(o):
        return (lax.rem(zh + o, NZ) * (NX * NY) + plane, f)

    loads = [
        pltpu.make_async_copy(x_hbm, xv, lsem.at[0]),
        pltpu.make_async_copy(g_hbm, gv, lsem.at[1]),
        pltpu.make_async_copy(mom_hbm, mv, lsem.at[2]),
    ]
    for copy in loads:
        copy.start()

    barrier = pltpu.get_barrier_semaphore()
    for make, count in ((line_peer, NF), (row_peer, NX), (col_peer, NY), (hi_peer, NZ)):
        for o in range(1, count):
            pl.semaphore_signal(barrier, inc=1, device_id=make(o), device_id_type=MESH)
    pl.semaphore_wait(barrier, NF + NX + NY + NZ - 4)

    sends = []

    def remote(src, dst, ssem, rsem, peer):
        copy = pltpu.make_async_remote_copy(
            src_ref=src, dst_ref=dst, send_sem=ssem, recv_sem=rsem,
            device_id=peer, device_id_type=MESH,
        )
        copy.start()
        sends.append(copy)
        return copy

    pk_copies = [
        remote(pk_ref, pk_all.at[f], pk_s.at[o - 1], pk_r.at[o - 1], line_peer(o))
        for o in range(1, NF)
    ]

    def send_x(slab):
        out = []
        for o in range(1, NF):
            peer = lax.rem(f + o, NF)
            cols = pl.ds(pl.multiple_of(peer * 1024 + slab * 256, 256), 256)
            k = slab * 3 + o - 1
            out.append(
                remote(
                    x_hbm.at[:, cols], xr.at[o - 1, :, pl.ds(slab * 256, 256)],
                    x_s.at[k], x_r.at[k], line_peer(o),
                )
            )
        return out

    x_copies = [send_x(0)]

    pk_all[f] = pk_ref[...]
    table = (ch_ref[...], cl_ref[...])
    loads[1].wait()
    gc = split(
        jnp.concatenate(
            [
                dot(gv[:, 256 * t : 256 * t + 256], table[0], 1, 1)
                + dot(gv[:, 256 * t : 256 * t + 256], table[1], 1, 1)
                for t in range(2)
            ],
            axis=1,
        )
    )
    for copy in pk_copies:
        copy.wait_recv()

    rows = iota((256, 128), 0)
    lane = iota((256, 128), 1)
    pick_lane = lane == ((rows >> 1) & 7)
    spread = (iota((256, 16), 1) == (iota((256, 16), 0) >> 4)).astype(BF)
    odd_row = (rows & 1).astype(F32)
    lane2 = iota((256, 256), 1).astype(F32)
    shift = (((iota((256, 1), 0) >> 4) & 3) * 64).astype(F32)
    loads[0].wait()
    for fi in range(NF):
        at = pl.ds(fi * 256, 256)
        number = jnp.sum(jnp.where(pick_lane, dot(spread, pk_all[fi]), 0.0), axis=1, keepdims=True)
        col = jnp.floor(number * (1.0 / 32.0))
        coeff_row = 2.0 * (number - 32.0 * col) + odd_row[:, :1]
        onehot = jnp.where(lane2 == coeff_row + shift, 1.0, 0.0).astype(BF)
        cs_high = dot(onehot, table[0]).astype(BF)
        cs_low = dot(onehot, table[1]).astype(BF)
        csh[at, :] = cs_high
        csl[at, :] = cs_low
        col_b = jnp.broadcast_to(col, (256, 128))
        jrow[at, :] = col_b
        trow[at, :] = jnp.broadcast_to(coeff_row + 64.0 * jnp.floor(col * 0.5), (256, 128))
        parts = []
        for s in range(SLABS):
            xs = xv[:, (fi * SLABS + s) * 256 : (fi * SLABS + s + 1) * 256]
            parts.append(
                dot(cs_high[64 * s : 64 * s + 64], xs, 1, 1)
                + dot(cs_low[64 * s : 64 * s + 64], xs, 1, 1)
            )
        value = dot3(split(jnp.concatenate(parts, axis=0)), gc)
        packed = pack(fold(value, col_b))
        upart[fi] = packed
        usend[fi] = packed.astype(BF)

    u_copies = [
        remote(
            usend.at[lax.rem(f + o, NF)], urecv.at[o - 1], u_s.at[o - 1], u_r.at[o - 1], line_peer(o)
        )
        for o in range(1, NF)
    ]
    x_copies.append(send_x(1))

    own = pl.multiple_of(f * 256, 256)
    loads[2].wait()
    parts = []
    for s in range(SLABS):
        high = csh[pl.ds(own + 64 * s, 64), :]
        low = csl[pl.ds(own + 64 * s, 64), :]
        ms = mv[256 * s : 256 * s + 256, :]
        parts.append(dot(high, ms) + dot(low, ms))
    col_b = jrow[pl.ds(own, 256), :]
    from_momentum = fold(lanes_transform(jnp.concatenate(parts, axis=0), table, 1), col_b)
    packed = upart[f] + 0.9 * pack(from_momentum)
    for copy in u_copies:
        copy.wait_recv()
    for o in range(3):
        packed = packed + urecv[o].astype(F32)
    packed = jnp.concatenate([packed, pltpu.roll(packed, 64, 1)], axis=0)
    col_odd = col_b - 2.0 * jnp.floor(col_b * 0.5)
    tile = jnp.where(lane < 64, packed, jnp.where(lane < 96, trow[pl.ds(own, 256), :], col_odd))
    sent[...] = tile.astype(BF)

    a_copies = []
    for o in range(1, NX):
        there = pl.ds(pl.multiple_of(lax.rem(m + o, NX) * 32, 32), 32)
        a_copies.append(
            remote(sent.at[there, :], a2.at[o - 1], a_s.at[o - 1], a_r.at[o - 1], row_peer(o))
        )
    a2[NX - 1] = sent[pl.ds(pl.multiple_of(m * 32, 32), 32), :]
    for copy in a_copies:
        copy.wait_recv()
    lane1 = iota((128, 128), 1)
    lane256 = iota((128, 256), 1).astype(F32)
    for u in range(2):
        got = jnp.concatenate(
            [a2[o, 16 * u : 16 * u + 16, :] for o in range(NX)], axis=0
        ).astype(F32)
        value = jnp.where(lane1 < 64, got, 0.0)
        value = value + pltpu.roll(value, 64, 1)
        value = jnp.where((lane1 >> 6).astype(F32) == got[:, 96:97], value, 0.0)
        onehot = jnp.where(lane256 == got[:, 64:65], 1.0, 0.0)
        dense = dot(onehot.astype(BF), value.astype(BF), 0, 0).astype(BF)
        for s in range(4):
            dp[4 * u + s] = dense[64 * s : 64 * s + 64]
    b_copies = [
        remote(
            dp.at[lax.rem(y + o, NY)], by.at[o - 1], b_s.at[o - 1], b_r.at[o - 1], col_peer(o)
        )
        for o in range(1, NY)
    ]
    plane_sum = dp[y].astype(F32)
    for copy in b_copies:
        copy.wait_recv()
    for o in range(NY - 1):
        plane_sum = plane_sum + by[o].astype(F32)
    zb[zh] = plane_sum.astype(BF)
    z_copies = [
        remote(zb.at[zh], zb.at[zh], z_s.at[o - 1], z_r.at[o - 1], hi_peer(o))
        for o in range(1, NZ)
    ]
    x_copies.append(send_x(2))
    x_copies.append(send_x(3))
    g_copies = [
        remote(g_hbm, gr.at[o - 1], g_s.at[o - 1], g_r.at[o - 1], line_peer(o))
        for o in range(1, NF)
    ]
    for copy in z_copies:
        copy.wait_recv()
    total = zb[0].astype(F32) + zb[1].astype(F32) + zb[2].astype(F32)
    left = dot3((cth_ref[:64, :64], ctl_ref[:64, :64]), split(total))
    piece = dot3(split(left), (ch_ref[:128, :128], cl_ref[:128, :128]))
    piece_rows = pl.ds(pl.multiple_of(m * 128 + lax.div(y, 4) * 64, 64), 64)
    piece_cols = pl.ds(pl.multiple_of(lax.rem(y, 4) * 128, 128), 128)
    fin[piece_rows, piece_cols] = piece.astype(BF)
    y_copies = [
        remote(
            fin.at[piece_rows, piece_cols], fin.at[piece_rows, piece_cols],
            y_s.at[o - 1], y_r.at[o - 1], col_peer(o),
        )
        for o in range(1, NY)
    ]
    for copy in y_copies:
        copy.wait_recv()
    band = pl.ds(pl.multiple_of(m * 128, 128), 128)
    w_copies = [
        remote(fin.at[band, :], fin.at[band, :], w_s.at[o - 1], w_r.at[o - 1], row_peer(2 * o))
        for o in range(1, 4)
    ]
    other = (row + m + 1 - 2 * lax.rem(m, 2), f)
    c_copies = [remote(fin.at[band, :], fin.at[band, :], c_s.at[0], c_r.at[0], other)]
    for o in range(1, 4):
        w_copies[o - 1].wait_recv()
        there = pl.ds(pl.multiple_of(lax.rem(m + NX - 2 * o, NX) * 128, 128), 128)
        c_copies.append(remote(fin.at[there, :], fin.at[there, :], c_s.at[o], c_r.at[o], other))
    for copy in c_copies:
        copy.wait_recv()
    u_out = pltpu.make_async_copy(fin, out_u, lsem.at[0])
    u_out.start()

    for copy in g_copies:
        copy.wait_recv()
    m_out = []
    lane512 = (iota((64, 512), 1) >> 6).astype(F32)
    for s in range(SLABS):
        for copy in x_copies[s]:
            copy.wait_recv()
        cols = pl.ds(pl.multiple_of(f * 1024 + s * 256, 256), 256)
        moment = 0.9 * mv[256 * s : 256 * s + 256, :].astype(F32)
        moment = moment + dot(xv[:, cols], gv[...], 0, 0)
        for o in range(NF - 1):
            moment = moment + dot(xr[o, :, 256 * s : 256 * s + 256], gr[o], 0, 0)
        cs = (csh[pl.ds(own + 64 * s, 64), :], csl[pl.ds(own + 64 * s, 64), :])
        coeff = lanes_transform(dot3(cs, split(moment)), table, 1)
        coeff = jnp.where(lane512 == jrow[pl.ds(own + 64 * s, 64), :1], coeff, 0.0)
        chosen = dot3(cs, split(lanes_transform(coeff, table, 0)), 0, 0)
        mout[256 * s : 256 * s + 256, :] = (moment - chosen).astype(BF)
        copy = pltpu.make_async_copy(
            mout.at[pl.ds(256 * s, 256), :], out_m.at[pl.ds(256 * s, 256), :], lsem.at[1 + s]
        )
        copy.start()
        m_out.append(copy)
    for copy in m_out:
        copy.wait()
    u_out.wait()
    for copy in sends:
        copy.wait_send()


def body(activations, output_grads, momentum, chosen_blocks):
    high, low = tables()
    picks = jnp.pad(chosen_blocks[0].astype(BF), ((0, 0), (0, 120)))
    dma = pltpu.SemaphoreType.DMA
    vmem = pl.BlockSpec(memory_space=pltpu.VMEM)
    anywhere = pl.BlockSpec(memory_space=pl.ANY)
    scratch = [
        pltpu.VMEM((256, 4096), BF),
        pltpu.VMEM((256, 512), BF),
        pltpu.VMEM((1024, 512), BF),
        pltpu.VMEM((3, 256, 1024), BF),
        pltpu.VMEM((3, 256, 512), BF),
        pltpu.VMEM((4, 16, 128), BF),
        pltpu.VMEM((1024, 256), BF),
        pltpu.VMEM((1024, 256), BF),
        pltpu.VMEM((1024, 128), F32),
        pltpu.VMEM((1024, 128), F32),
        pltpu.VMEM((4, 128, 128), F32),
        pltpu.VMEM((4, 128, 128), BF),
        pltpu.VMEM((3, 128, 128), BF),
        pltpu.VMEM((256, 128), BF),
        pltpu.VMEM((8, 32, 128), BF),
        pltpu.VMEM((8, 64, 128), BF),
        pltpu.VMEM((7, 64, 128), BF),
        pltpu.VMEM((3, 64, 128), BF),
        pltpu.VMEM((1024, 512), BF),
        pltpu.VMEM((1024, 512), BF),
        dma((5,)),
        dma((3,)), dma((3,)), dma((12,)), dma((12,)), dma((3,)), dma((3,)),
        dma((3,)), dma((3,)), dma((7,)), dma((7,)), dma((7,)), dma((7,)),
        dma((2,)), dma((2,)), dma((7,)), dma((7,)), dma((3,)), dma((3,)),
        dma((4,)), dma((4,)),
    ]
    moment_next, update = pl.pallas_call(
        kernel,
        out_shape=(
            jax.ShapeDtypeStruct((1024, 512), BF),
            jax.ShapeDtypeStruct((1024, 512), BF),
        ),
        in_specs=[anywhere, anywhere, anywhere, vmem, vmem, vmem, vmem, vmem],
        out_specs=(anywhere, anywhere),
        scratch_shapes=scratch,
        compiler_params=pltpu.CompilerParams(
            collective_id=0, has_side_effects=True, vmem_limit_bytes=48 * 1024 * 1024
        ),
        name="step",
    )(
        activations, output_grads, momentum[0], picks,
        jnp.asarray(high), jnp.asarray(low), jnp.asarray(high.T), jnp.asarray(low.T),
    )
    return (moment_next[None], update.astype(F32))


def solution(mesh):
    return jax.shard_map(
        body,
        mesh=mesh,
        in_specs=(
            P(("replica", "fsdp"), None),
            P(("replica", "fsdp"), None),
            P("replica", "fsdp", None),
            P("replica", "fsdp", None),
        ),
        out_specs=(P("replica", "fsdp", None), P("fsdp", None)),
        check_vma=False,
    )
```

time: 542 us -> 116 us (0.21)
  the two profiles are of different devices: /device:TPU:1 before, /device:TPU:64 now
where the time goes in v1:
time: 116 us; the launch traced here: 115 us
  Pallas kernels  104 us (90%)
  local copies, waits for them, and re-layouts  8.44 us (7%)
  other arithmetic  2.3 us (2%)
    pallas_call x1, Pallas kernels, body(): pl.pallas_call(kernel, out_shape=(jax.ShapeDtypeStruct((1024, 512), BF),...  104 us
    unnamed x15, local copies, waits for them, and re-layouts  8.35 us

profile of v1, /device:TPU:64, one launch (start us, length us, event | category | flops | bytes accessed | tf_op | source)
XLA Modules:
  0.0 115.3 jit_solution(1786700171903402028)
XLA Ops:
  0.6 0.7 convert_bitcast_fusion
  1.3 0.1 copy.10
  1.4 0.0 copy-start
  1.4 1.6 %copy-done = bf16[256,4096]{1,0:T(8,128)(2,1)S(1)} copy-done((bf16[256,4096]{1,0:T(8,128)(2,1)S(1)}, bf16[256,4096]{1,0:T(8,128)(2,1)}, u32[]{:S(2)}) %copy-start) | copy-done | bytes 2097176
  3.0 0.0 copy-start.1
  3.0 1.2 %copy-done.1 = bf16[1,1024,512]{2,1,0:T(8,128)(2,1)S(1)} copy-done((bf16[1,1024,512]{2,1,0:T(8,128)(2,1)S(1)}, bf16[1,1024,512]{2,1,0:T(8,128)(2,1)}, u32[]{:S(2)}) %copy-start.1) | copy-done | bytes 1048600
  4.2 0.0 copy-start.2
  4.2 0.9 copy-done.2
  5.2 0.0 copy-start.3
  5.2 0.9 copy-done.3
  6.1 0.0 copy-start.4
  6.1 0.9 copy-done.4
  7.0 0.0 copy-start.5
  7.0 0.9 copy-done.5
  7.9 0.0 copy-start.6
  7.9 0.9 copy-done.6
  8.8 103.9 %step.1 = (bf16[1024,512]{1,0:T(8,128)(2,1)S(1)}, bf16[1024,512]{1,0:T(8,128)(2,1)S(1)}) custom-call(bf16[256,4096]{1,0:T(8,128)(2,1)S(1)} %copy-done, bf16[256,512]{1,0:T(8,128)(2,1)S(1)} %copy-done.2, bf16[1024,512]{1,0:T(8,128)(2,1)S(1)} %bitcast.4, bf16[16,128]{1,0:T(8,128)(2,1)S(1)} %pad.4.pk_ref, bf16[256,256]{1,0:T(8,128)(2,1)S(1)} %copy-done.6, ...), custom_call_target="tpu_custom_call" | custom-call | tf_op jit(solution)/shard_map/step/pallas_call | solution.py:365
  112.7 1.6 %convert_element_type.13 = f32[1024,512]{1,0:T(8,128)} convert(bf16[1024,512]{1,0:T(8,128)(2,1)S(1)} %get-tuple-element.5) | non-fusion elementwise | flops 524288 | bytes 3145728 | tf_op jit(solution)/shard_map/convert_element_type | solution.py:382
  114.3 1.0 copy.12
  (1 shorter events, 0.0 us)
Async XLA Ops:
  1.4 1.6 %copy-start = (bf16[256,4096]{1,0:T(8,128)(2,1)S(1)}, bf16[256,4096]{1,0:T(8,128)(2,1)}, u32[]{:S(2)}) copy-start(bf16[256,4096]{1,0:T(8,128)(2,1)} %x_hbm.1) | copy-start | bytes 6291460
  3.0 1.2 %copy-start.1 = (bf16[1,1024,512]{2,1,0:T(8,128)(2,1)S(1)}, bf16[1,1024,512]{2,1,0:T(8,128)(2,1)}, u32[]{:S(2)}) copy-start(bf16[1,1024,512]{2,1,0:T(8,128)(2,1)} %param.10) | copy-start | bytes 3145732
  4.2 0.9 copy-start.2
  5.2 0.9 copy-start.3
  6.1 0.9 copy-start.4
  7.0 0.9 copy-start.5
  7.9 0.9 copy-start.6

commit v2 on v1

--- a/solution.py
+++ b/solution.py
@@ -14,6 +14,7 @@
 SPAN = 64
 NX, NY, NZ, NF = 8, 8, 3, 4
 SLABS = 4
+PIECES = 8
 
 
 def tables():
@@ -73,10 +74,10 @@
 
 
 def kernel(
-    x_hbm, g_hbm, mom_hbm, pk_ref, ch_ref, cl_ref, cth_ref, ctl_ref,
+    x_hbm, g_hbm, mom_hbm, pk_hbm, tab_hbm,
     out_m, out_u,
-    xv, gv, mv, xr, gr, pk_all, csh, csl, jrow, trow, upart, usend, urecv,
-    sent, a2, dp, by, zb, fin, mout,
+    xv, g_all, mv, tab, xr, pk_all, csh, csl, jrow, trow, upart, usend, urecv,
+    sent, a2, dp, by, zb, fin,
     lsem, pk_s, pk_r, x_s, x_r, g_s, g_r, u_s, u_r, a_s, a_r, b_s, b_r,
     z_s, z_r, y_s, y_r, w_s, w_r, c_s, c_r,
 ):
@@ -102,8 +103,10 @@
 
     loads = [
         pltpu.make_async_copy(x_hbm, xv, lsem.at[0]),
-        pltpu.make_async_copy(g_hbm, gv, lsem.at[1]),
-        pltpu.make_async_copy(mom_hbm, mv, lsem.at[2]),
+        pltpu.make_async_copy(g_hbm, g_all.at[f], lsem.at[1]),
+        pltpu.make_async_copy(mom_hbm.at[0], mv, lsem.at[2]),
+        pltpu.make_async_copy(tab_hbm, tab, lsem.at[3]),
+        pltpu.make_async_copy(pk_hbm, pk_all.at[f], lsem.at[4]),
     ]
     for copy in loads:
         copy.start()
@@ -126,29 +129,69 @@
         return copy
 
     pk_copies = [
-        remote(pk_ref, pk_all.at[f], pk_s.at[o - 1], pk_r.at[o - 1], line_peer(o))
+        remote(pk_hbm, pk_all.at[f], pk_s.at[o - 1], pk_r.at[o - 1], line_peer(o))
         for o in range(1, NF)
     ]
 
-    def send_x(slab):
-        out = []
-        for o in range(1, NF):
-            peer = lax.rem(f + o, NF)
-            cols = pl.ds(pl.multiple_of(peer * 1024 + slab * 256, 256), 256)
-            k = slab * 3 + o - 1
-            out.append(
-                remote(
-                    x_hbm.at[:, cols], xr.at[o - 1, :, pl.ds(slab * 256, 256)],
-                    x_s.at[k], x_r.at[k], line_peer(o),
+    x_copies = []
+
+    def send_x(count):
+        for piece in range(len(x_copies), len(x_copies) + count):
+            out = []
+            for o in range(1, NF):
+                peer = lax.rem(f + o, NF)
+                cols = pl.ds(pl.multiple_of(peer * 1024 + piece * 128, 128), 128)
+                k = piece * 3 + o - 1
+                out.append(
+                    remote(
+                        x_hbm.at[:, cols], xr.at[o - 1, :, pl.ds(piece * 128, 128)],
+                        x_s.at[k], x_r.at[k], line_peer(o),
+                    )
                 )
-            )
-        return out
-
-    x_copies = [send_x(0)]
-
-    pk_all[f] = pk_ref[...]
-    table = (ch_ref[...], cl_ref[...])
-    loads[1].wait()
+            x_copies.append(out)
+
+    def relay(hop, direction):
+        step = 1 - 2 * direction
+        source = f - step * hop
+        present = (source >= 0) & (source < NF)
+        onward = present & (f + step >= 0) & (f + step < NF)
+        slot = lax.rem(source + NF, NF)
+        copy = pltpu.make_async_remote_copy(
+            src_ref=g_all.at[slot], dst_ref=g_all.at[slot],
+            send_sem=g_s.at[direction * 3 + lax.rem(hop, 3)], recv_sem=g_r.at[direction * 3 + hop],
+            device_id=(rep, lax.rem(f + step + NF, NF)), device_id_type=MESH,
+        )
+        return present, onward, copy
+
+    def send_g(hop):
+        for direction in range(2):
+            _, onward, copy = relay(hop, direction)
+
+            @pl.when(onward)
+            def _():
+                copy.start()
+
+    def wait_g(hop):
+        for direction in range(2):
+            step = 1 - 2 * direction
+            source = f - step * hop
+            slot = lax.rem(source + NF, NF)
+
+            @pl.when((source >= 0) & (source < NF))
+            def _():
+                pltpu.make_async_remote_copy(
+                    src_ref=g_all.at[slot], dst_ref=g_all.at[slot],
+                    send_sem=g_s.at[direction * 3], recv_sem=g_r.at[direction * 3 + hop - 1],
+                    device_id=(rep, lax.rem(f + step + NF, NF)), device_id_type=MESH,
+                ).wait_recv()
+
+
+    for copy in (loads[1], loads[3], loads[4]):
+        copy.wait()
+    send_g(0)
+    send_x(1)
+    table = (tab[0], tab[1])
+    gv = g_all[f]
     gc = split(
         jnp.concatenate(
             [
@@ -201,7 +244,9 @@
         )
         for o in range(1, NF)
     ]
-    x_copies.append(send_x(1))
+    wait_g(1)
+    send_g(1)
+    send_x(2)
 
     own = pl.multiple_of(f * 256, 256)
     loads[2].wait()
@@ -261,17 +306,14 @@
         remote(zb.at[zh], zb.at[zh], z_s.at[o - 1], z_r.at[o - 1], hi_peer(o))
         for o in range(1, NZ)
     ]
-    x_copies.append(send_x(2))
-    x_copies.append(send_x(3))
-    g_copies = [
-        remote(g_hbm, gr.at[o - 1], g_s.at[o - 1], g_r.at[o - 1], line_peer(o))
-        for o in range(1, NF)
-    ]
+    wait_g(2)
+    send_g(2)
+    send_x(5)
     for copy in z_copies:
         copy.wait_recv()
     total = zb[0].astype(F32) + zb[1].astype(F32) + zb[2].astype(F32)
-    left = dot3((cth_ref[:64, :64], ctl_ref[:64, :64]), split(total))
-    piece = dot3(split(left), (ch_ref[:128, :128], cl_ref[:128, :128]))
+    left = dot3((tab[2, :64, :64], tab[3, :64, :64]), split(total))
+    piece = dot3(split(left), (tab[0, :128, :128], tab[1, :128, :128]))
     piece_rows = pl.ds(pl.multiple_of(m * 128 + lax.div(y, 4) * 64, 64), 64)
     piece_cols = pl.ds(pl.multiple_of(lax.rem(y, 4) * 128, 128), 128)
     fin[piece_rows, piece_cols] = piece.astype(BF)
@@ -282,6 +324,24 @@
         )
         for o in range(1, NY)
     ]
+    lane512 = (iota((64, 512), 1) >> 6).astype(F32)
+
+    def slab(s):
+        for piece in (2 * s, 2 * s + 1):
+            for copy in x_copies[piece]:
+                copy.wait_recv()
+        cols = pl.ds(pl.multiple_of(f * 1024 + s * 256, 256), 256)
+        moment = 0.9 * mv[256 * s : 256 * s + 256, :].astype(F32)
+        moment = moment + dot(xv[:, cols], g_all[f], 0, 0)
+        for o in range(1, NF):
+            source = lax.rem(f + NF - o, NF)
+            moment = moment + dot(xr[o - 1, :, 256 * s : 256 * s + 256], g_all[source], 0, 0)
+        cs = (csh[pl.ds(own + 64 * s, 64), :], csl[pl.ds(own + 64 * s, 64), :])
+        coeff = lanes_transform(dot3(cs, split(moment)), table, 1)
+        coeff = jnp.where(lane512 == jrow[pl.ds(own + 64 * s, 64), :1], coeff, 0.0)
+        chosen = dot3(cs, split(lanes_transform(coeff, table, 0)), 0, 0)
+        out_m[256 * s : 256 * s + 256, :] = (moment - chosen).astype(BF)
+
     for copy in y_copies:
         copy.wait_recv()
     band = pl.ds(pl.multiple_of(m * 128, 128), 128)
@@ -291,56 +351,41 @@
     ]
     other = (row + m + 1 - 2 * lax.rem(m, 2), f)
     c_copies = [remote(fin.at[band, :], fin.at[band, :], c_s.at[0], c_r.at[0], other)]
+    wait_g(3)
+    slab(0)
     for o in range(1, 4):
         w_copies[o - 1].wait_recv()
         there = pl.ds(pl.multiple_of(lax.rem(m + NX - 2 * o, NX) * 128, 128), 128)
         c_copies.append(remote(fin.at[there, :], fin.at[there, :], c_s.at[o], c_r.at[o], other))
+    slab(1)
     for copy in c_copies:
         copy.wait_recv()
-    u_out = pltpu.make_async_copy(fin, out_u, lsem.at[0])
-    u_out.start()
-
-    for copy in g_copies:
-        copy.wait_recv()
-    m_out = []
-    lane512 = (iota((64, 512), 1) >> 6).astype(F32)
-    for s in range(SLABS):
-        for copy in x_copies[s]:
-            copy.wait_recv()
-        cols = pl.ds(pl.multiple_of(f * 1024 + s * 256, 256), 256)
-        moment = 0.9 * mv[256 * s : 256 * s + 256, :].astype(F32)
-        moment = moment + dot(xv[:, cols], gv[...], 0, 0)
-        for o in range(NF - 1):
-            moment = moment + dot(xr[o, :, 256 * s : 256 * s + 256], gr[o], 0, 0)
-        cs = (csh[pl.ds(own + 64 * s, 64), :], csl[pl.ds(own + 64 * s, 64), :])
-        coeff = lanes_transform(dot3(cs, split(moment)), table, 1)
-        coeff = jnp.where(lane512 == jrow[pl.ds(own + 64 * s, 64), :1], coeff, 0.0)
-        chosen = dot3(cs, split(lanes_transform(coeff, table, 0)), 0, 0)
-        mout[256 * s : 256 * s + 256, :] = (moment - chosen).astype(BF)
-        copy = pltpu.make_async_copy(
-            mout.at[pl.ds(256 * s, 256), :], out_m.at[pl.ds(256 * s, 256), :], lsem.at[1 + s]
-        )
-        copy.start()
-        m_out.append(copy)
-    for copy in m_out:
-        copy.wait()
-    u_out.wait()
+    out_u[...] = fin[...]
+
+    slab(2)
+    slab(3)
     for copy in sends:
         copy.wait_send()
+    for hop in range(3):
+        for direction in range(2):
+            _, onward, copy = relay(hop, direction)
+
+            @pl.when(onward)
+            def _():
+                copy.wait_send()
 
 
 def body(activations, output_grads, momentum, chosen_blocks):
     high, low = tables()
     picks = jnp.pad(chosen_blocks[0].astype(BF), ((0, 0), (0, 120)))
     dma = pltpu.SemaphoreType.DMA
-    vmem = pl.BlockSpec(memory_space=pltpu.VMEM)
     anywhere = pl.BlockSpec(memory_space=pl.ANY)
     scratch = [
         pltpu.VMEM((256, 4096), BF),
-        pltpu.VMEM((256, 512), BF),
+        pltpu.VMEM((4, 256, 512), BF),
         pltpu.VMEM((1024, 512), BF),
+        pltpu.VMEM((4, 256, 256), BF),
         pltpu.VMEM((3, 256, 1024), BF),
-        pltpu.VMEM((3, 256, 512), BF),
         pltpu.VMEM((4, 16, 128), BF),
         pltpu.VMEM((1024, 256), BF),
         pltpu.VMEM((1024, 256), BF),
@@ -355,9 +400,8 @@
         pltpu.VMEM((7, 64, 128), BF),
         pltpu.VMEM((3, 64, 128), BF),
         pltpu.VMEM((1024, 512), BF),
-        pltpu.VMEM((1024, 512), BF),
         dma((5,)),
-        dma((3,)), dma((3,)), dma((12,)), dma((12,)), dma((3,)), dma((3,)),
+        dma((3,)), dma((3,)), dma((24,)), dma((24,)), dma((6,)), dma((6,)),
         dma((3,)), dma((3,)), dma((7,)), dma((7,)), dma((7,)), dma((7,)),
         dma((2,)), dma((2,)), dma((7,)), dma((7,)), dma((3,)), dma((3,)),
         dma((4,)), dma((4,)),
@@ -368,16 +412,16 @@
             jax.ShapeDtypeStruct((1024, 512), BF),
             jax.ShapeDtypeStruct((1024, 512), BF),
         ),
-        in_specs=[anywhere, anywhere, anywhere, vmem, vmem, vmem, vmem, vmem],
-        out_specs=(anywhere, anywhere),
+        in_specs=[anywhere] * 5,
+        out_specs=(pl.BlockSpec(memory_space=pltpu.VMEM),) * 2,
         scratch_shapes=scratch,
         compiler_params=pltpu.CompilerParams(
-            collective_id=0, has_side_effects=True, vmem_limit_bytes=48 * 1024 * 1024
+            collective_id=0, has_side_effects=True, vmem_limit_bytes=62 * 1024 * 1024
         ),
         name="step",
     )(
-        activations, output_grads, momentum[0], picks,
-        jnp.asarray(high), jnp.asarray(low), jnp.asarray(high.T), jnp.asarray(low.T),
+        activations, output_grads, momentum, picks,
+        jnp.asarray(np.stack([high, low, high.T, low.T])),
     )
     return (moment_next[None], update.astype(F32))
 

time: 116 us -> 89 us (0.77)
  the two profiles are of different devices: /device:TPU:64 before, /device:TPU:1 now
where the time goes in v2:
time: 89 us; the launch traced here: 88.8 us
  Pallas kernels  82.9 us (93%)
  other arithmetic  3.61 us (4%)
  local copies, waits for them, and re-layouts  1.66 us (2%)
    pallas_call x1, Pallas kernels, body(): pl.pallas_call(kernel, out_shape=(jax.ShapeDtypeStruct((1024, 512), BF),...  82.9 us
    convert_element_type x1, other arithmetic, body(): return (moment_next[None], update.astype(F32))  2.92 us

profile of v2, /device:TPU:1, one launch (start us, length us, event | category | flops | bytes accessed | tf_op | source)
XLA Modules:
  0.0 88.8 jit_solution(13045749525225055028)
XLA Ops:
  0.6 0.7 convert_bitcast_fusion
  1.3 0.1 copy.7
  1.4 0.6 pad.4.pk_hbm
  2.0 82.9 %step.1 = (bf16[1024,512]{1,0:T(8,128)(2,1)}, bf16[1024,512]{1,0:T(8,128)(2,1)}) custom-call(bf16[256,4096]{1,0:T(8,128)(2,1)} %x_hbm.1, bf16[256,512]{1,0:T(8,128)(2,1)} %g_hbm.1, bf16[1,1024,512]{2,1,0:T(8,128)(2,1)} %mom_hbm.1, bf16[16,128]{1,0:T(8,128)(2,1)} %pad.4.pk_hbm, bf16[4,256,256]{2,1,0:T(8,128)(2,1)} %constant.5.clone.tab_hbm), custom_call_target="tpu_custom_call" | custom-call | tf_op jit(solution)/shard_map/step/pallas_call | solution.py:409
  84.9 0.0 copy-start
  84.9 2.9 %convert_element_type.13 = f32[1024,512]{1,0:T(8,128)} convert(bf16[1024,512]{1,0:T(8,128)(2,1)} %get-tuple-element.5) | non-fusion elementwise | flops 524288 | bytes 3145728 | tf_op jit(solution)/shard_map/convert_element_type | solution.py:426
  87.8 0.0 copy-done
  87.8 1.0 %copy.9 = bf16[1,1024,512]{2,1,0:T(8,128)(2,1)} copy(bf16[1,1024,512]{2,1,0:T(8,128)(2,1)S(1)} %bitcast.3) | data formatting | bytes 2097152
Async XLA Ops:
  84.9 2.9 %copy-start = (bf16[1024,512]{1,0:T(8,128)(2,1)S(1)}, bf16[1024,512]{1,0:T(8,128)(2,1)}, u32[]{:S(2)}) copy-start(bf16[1024,512]{1,0:T(8,128)(2,1)} %get-tuple-element.4) | copy-start | bytes 3145732

commit v3 on v2

--- a/solution.py
+++ b/solution.py
@@ -76,9 +76,9 @@
 def kernel(
     x_hbm, g_hbm, mom_hbm, pk_hbm, tab_hbm,
     out_m, out_u,
-    xv, g_all, mv, tab, xr, pk_all, csh, csl, jrow, trow, upart, usend, urecv,
+    xv, g_all, mv, tab, xr, pk_own, pk_all, csh, csl, jrow, trow, upart, usend, urecv,
     sent, a2, dp, by, zb, fin,
-    lsem, pk_s, pk_r, x_s, x_r, g_s, g_r, u_s, u_r, a_s, a_r, b_s, b_r,
+    gate, lsem, pk_s, pk_r, x_s, x_r, g_s, g_r, u_s, u_r, a_s, a_r, b_s, b_r,
     z_s, z_r, y_s, y_r, w_s, w_r, c_s, c_r,
 ):
     rep = lax.axis_index("replica")
@@ -106,16 +106,44 @@
         pltpu.make_async_copy(g_hbm, g_all.at[f], lsem.at[1]),
         pltpu.make_async_copy(mom_hbm.at[0], mv, lsem.at[2]),
         pltpu.make_async_copy(tab_hbm, tab, lsem.at[3]),
-        pltpu.make_async_copy(pk_hbm, pk_all.at[f], lsem.at[4]),
+        pltpu.make_async_copy(pk_hbm, pk_own, lsem.at[4]),
     ]
     for copy in loads:
         copy.start()
 
     barrier = pltpu.get_barrier_semaphore()
-    for make, count in ((line_peer, NF), (row_peer, NX), (col_peer, NY), (hi_peer, NZ)):
-        for o in range(1, count):
-            pl.semaphore_signal(barrier, inc=1, device_id=make(o), device_id_type=MESH)
-    pl.semaphore_wait(barrier, NF + NX + NY + NZ - 4)
+    core = lax.rem(m, 2)
+    other = (rep + 1 - 2 * core, f)
+
+    def enter(there):
+        pl.semaphore_signal(barrier, inc=1, device_id=there, device_id_type=MESH)
+
+    for o in range(1, NF):
+        enter((rep - core, lax.rem(f + o, NF)))
+    for o in range(2, NX, 2):
+        enter((row + lax.rem(m - core + o, NX), f))
+    for o in range(1, NY):
+        enter((zh * (NX * NY) + lax.rem(y + o, NY) * NX + m - core, f))
+    for o in range(1, NZ):
+        enter((lax.rem(zh + o, NZ) * (NX * NY) + plane - core + 1, f))
+
+    @pl.when(core == 1)
+    def _():
+        enter(other)
+
+    for copy in (loads[4],):
+        copy.wait()
+    pk_all[f] = jnp.zeros((8, 128), F32)
+    pk_all[f, :, :16] = pk_own[...].astype(F32)
+
+    @pl.when(core == 0)
+    def _():
+        pl.semaphore_wait(barrier, 2 * (NF - 1) + (NX - 1) + 2 * (NY - 1))
+        pl.semaphore_signal(gate, inc=1, device_id=other, device_id_type=MESH)
+
+    @pl.when(core == 1)
+    def _():
+        pl.semaphore_wait(gate, 1)
 
     sends = []
 
@@ -129,7 +157,7 @@
         return copy
 
     pk_copies = [
-        remote(pk_hbm, pk_all.at[f], pk_s.at[o - 1], pk_r.at[o - 1], line_peer(o))
+        remote(pk_all.at[f], pk_all.at[f], pk_s.at[o - 1], pk_r.at[o - 1], line_peer(o))
         for o in range(1, NF)
     ]
 
@@ -186,7 +214,7 @@
                 ).wait_recv()
 
 
-    for copy in (loads[1], loads[3], loads[4]):
+    for copy in (loads[1], loads[3]):
         copy.wait()
     send_g(0)
     send_x(1)
@@ -207,15 +235,15 @@
 
     rows = iota((256, 128), 0)
     lane = iota((256, 128), 1)
-    pick_lane = lane == ((rows >> 1) & 7)
-    spread = (iota((256, 16), 1) == (iota((256, 16), 0) >> 4)).astype(BF)
+    pick_lane = lane == (rows >> 4)
+    spread = (iota((256, 8), 1) == ((iota((256, 8), 0) >> 1) & 7)).astype(BF)
     odd_row = (rows & 1).astype(F32)
     lane2 = iota((256, 256), 1).astype(F32)
     shift = (((iota((256, 1), 0) >> 4) & 3) * 64).astype(F32)
     loads[0].wait()
     for fi in range(NF):
         at = pl.ds(fi * 256, 256)
-        number = jnp.sum(jnp.where(pick_lane, dot(spread, pk_all[fi]), 0.0), axis=1, keepdims=True)
+        number = jnp.sum(jnp.where(pick_lane, dot(spread, pk_all[fi].astype(BF)), 0.0), axis=1, keepdims=True)
         col = jnp.floor(number * (1.0 / 32.0))
         coeff_row = 2.0 * (number - 32.0 * col) + odd_row[:, :1]
         onehot = jnp.where(lane2 == coeff_row + shift, 1.0, 0.0).astype(BF)
@@ -302,6 +330,16 @@
     for o in range(NY - 1):
         plane_sum = plane_sum + by[o].astype(F32)
     zb[zh] = plane_sum.astype(BF)
+
+    @pl.when(core == 1)
+    def _():
+        pl.semaphore_wait(barrier, 2 * (NZ - 1))
+        pl.semaphore_signal(gate, inc=1, device_id=other, device_id_type=MESH)
+
+    @pl.when(core == 0)
+    def _():
+        pl.semaphore_wait(gate, 1)
+
     z_copies = [
         remote(zb.at[zh], zb.at[zh], z_s.at[o - 1], z_r.at[o - 1], hi_peer(o))
         for o in range(1, NZ)
@@ -349,7 +387,6 @@
         remote(fin.at[band, :], fin.at[band, :], w_s.at[o - 1], w_r.at[o - 1], row_peer(2 * o))
         for o in range(1, 4)
     ]
-    other = (row + m + 1 - 2 * lax.rem(m, 2), f)
     c_copies = [remote(fin.at[band, :], fin.at[band, :], c_s.at[0], c_r.at[0], other)]
     wait_g(3)
     slab(0)
@@ -377,7 +414,7 @@
 
 def body(activations, output_grads, momentum, chosen_blocks):
     high, low = tables()
-    picks = jnp.pad(chosen_blocks[0].astype(BF), ((0, 0), (0, 120)))
+    picks = chosen_blocks[0].T
     dma = pltpu.SemaphoreType.DMA
     anywhere = pl.BlockSpec(memory_space=pl.ANY)
     scratch = [
@@ -386,7 +423,8 @@
         pltpu.VMEM((1024, 512), BF),
         pltpu.VMEM((4, 256, 256), BF),
         pltpu.VMEM((3, 256, 1024), BF),
-        pltpu.VMEM((4, 16, 128), BF),
+        pltpu.VMEM((8, 16), jnp.int32),
+        pltpu.VMEM((4, 8, 128), F32),
         pltpu.VMEM((1024, 256), BF),
         pltpu.VMEM((1024, 256), BF),
         pltpu.VMEM((1024, 128), F32),
@@ -400,6 +438,7 @@
         pltpu.VMEM((7, 64, 128), BF),
         pltpu.VMEM((3, 64, 128), BF),
         pltpu.VMEM((1024, 512), BF),
+        pltpu.SemaphoreType.REGULAR,
         dma((5,)),
         dma((3,)), dma((3,)), dma((24,)), dma((24,)), dma((6,)), dma((6,)),
         dma((3,)), dma((3,)), dma((7,)), dma((7,)), dma((7,)), dma((7,)),

time: 89 us -> 84.8 us (0.953); the launches traced: 88.8 us -> 83.2 us
  Pallas kernels: 82.9 us -> 78.6 us
    pallas_call x1, Pallas kernels: 82.9 us -> 78.6 us  [body(): pl.pallas_call(kernel, out_shape=(jax.ShapeDtypeStruct((1024, 512), BF),...]
where the time goes in v3:
time: 84.8 us; the launch traced here: 83.2 us
  Pallas kernels  78.6 us (93%)
  other arithmetic  2.92 us (3%)
  local copies, waits for them, and re-layouts  0.97 us (1%)
    pallas_call x1, Pallas kernels, body(): pl.pallas_call(kernel, out_shape=(jax.ShapeDtypeStruct((1024, 512), BF),...  78.6 us
    convert_element_type x1, other arithmetic, body(): return (moment_next[None], update.astype(F32))  2.92 us

profile of v3, /device:TPU:1, one launch (start us, length us, event | category | flops | bytes accessed | tf_op | source)
XLA Modules:
  0.0 83.2 jit_solution(827434154638218821)
XLA Ops:
  0.6 78.6 %step.1 = (bf16[1024,512]{1,0:T(8,128)(2,1)}, bf16[1024,512]{1,0:T(8,128)(2,1)}) custom-call(bf16[256,4096]{1,0:T(8,128)(2,1)} %x_hbm.1, bf16[256,512]{1,0:T(8,128)(2,1)} %g_hbm.1, bf16[1,1024,512]{2,1,0:T(8,128)(2,1)} %mom_hbm.1, s32[8,16]{1,0:T(8,128)} %bitcast.5, bf16[4,256,256]{2,1,0:T(8,128)(2,1)} %constant.2.clone.tab_hbm), custom_call_target="tpu_custom_call" | custom-call | tf_op jit(solution)/shard_map/step/pallas_call | solution.py:448
  79.3 0.0 copy-start
  79.3 2.9 %convert_element_type.3 = f32[1024,512]{1,0:T(8,128)} convert(bf16[1024,512]{1,0:T(8,128)(2,1)} %get-tuple-element.5) | non-fusion elementwise | flops 524288 | bytes 3145728 | tf_op jit(solution)/shard_map/convert_element_type | solution.py:465
  82.2 0.0 copy-done
  82.2 1.0 %copy.8 = bf16[1,1024,512]{2,1,0:T(8,128)(2,1)} copy(bf16[1,1024,512]{2,1,0:T(8,128)(2,1)S(1)} %bitcast.4) | data formatting | bytes 2097152
Async XLA Ops:
  79.3 2.9 %copy-start = (bf16[1024,512]{1,0:T(8,128)(2,1)S(1)}, bf16[1024,512]{1,0:T(8,128)(2,1)}, u32[]{:S(2)}) copy-start(bf16[1024,512]{1,0:T(8,128)(2,1)} %get-tuple-element.4) | copy-start | bytes 3145732

commit v4 on v3

--- a/solution.py
+++ b/solution.py
@@ -77,7 +77,7 @@
     x_hbm, g_hbm, mom_hbm, pk_hbm, tab_hbm,
     out_m, out_u,
     xv, g_all, mv, tab, xr, pk_own, pk_all, csh, csl, jrow, trow, upart, usend, urecv,
-    sent, a2, dp, by, zb, fin,
+    sent, a2, dp, by, zb, fin, mout,
     gate, lsem, pk_s, pk_r, x_s, x_r, g_s, g_r, u_s, u_r, a_s, a_r, b_s, b_r,
     z_s, z_r, y_s, y_r, w_s, w_r, c_s, c_r,
 ):
@@ -161,22 +161,24 @@
         for o in range(1, NF)
     ]
 
-    x_copies = []
-
-    def send_x(count):
-        for piece in range(len(x_copies), len(x_copies) + count):
-            out = []
-            for o in range(1, NF):
+    x_copies = [[] for _ in range(PIECES)]
+
+    def send_x(pieces, offsets=None):
+        for piece in pieces:
+            for step in range(NF - 1) if offsets is None else offsets:
+                o = step
+                if offsets is None:
+                    target = step + 1 - lax.div(f + NF - 1 - step, NF)
+                    o = lax.rem(target - f + NF, NF)
                 peer = lax.rem(f + o, NF)
                 cols = pl.ds(pl.multiple_of(peer * 1024 + piece * 128, 128), 128)
                 k = piece * 3 + o - 1
-                out.append(
+                x_copies[piece].append(
                     remote(
                         x_hbm.at[:, cols], xr.at[o - 1, :, pl.ds(piece * 128, 128)],
                         x_s.at[k], x_r.at[k], line_peer(o),
                     )
                 )
-            x_copies.append(out)
 
     def relay(hop, direction):
         step = 1 - 2 * direction
@@ -217,7 +219,7 @@
     for copy in (loads[1], loads[3]):
         copy.wait()
     send_g(0)
-    send_x(1)
+    send_x([0])
     table = (tab[0], tab[1])
     gv = g_all[f]
     gc = split(
@@ -230,8 +232,6 @@
             axis=1,
         )
     )
-    for copy in pk_copies:
-        copy.wait_recv()
 
     rows = iota((256, 128), 0)
     lane = iota((256, 128), 1)
@@ -240,60 +240,61 @@
     odd_row = (rows & 1).astype(F32)
     lane2 = iota((256, 256), 1).astype(F32)
     shift = (((iota((256, 1), 0) >> 4) & 3) * 64).astype(F32)
-    loads[0].wait()
-    for fi in range(NF):
-        at = pl.ds(fi * 256, 256)
-        number = jnp.sum(jnp.where(pick_lane, dot(spread, pk_all[fi].astype(BF)), 0.0), axis=1, keepdims=True)
+
+    def chosen_rows(fi):
+        picks = dot(spread, pk_all[fi].astype(BF))
+        number = jnp.sum(jnp.where(pick_lane, picks, 0.0), axis=1, keepdims=True)
         col = jnp.floor(number * (1.0 / 32.0))
         coeff_row = 2.0 * (number - 32.0 * col) + odd_row[:, :1]
         onehot = jnp.where(lane2 == coeff_row + shift, 1.0, 0.0).astype(BF)
-        cs_high = dot(onehot, table[0]).astype(BF)
-        cs_low = dot(onehot, table[1]).astype(BF)
-        csh[at, :] = cs_high
-        csl[at, :] = cs_low
-        col_b = jnp.broadcast_to(col, (256, 128))
-        jrow[at, :] = col_b
-        trow[at, :] = jnp.broadcast_to(coeff_row + 64.0 * jnp.floor(col * 0.5), (256, 128))
+        return dot(onehot, table[0]).astype(BF), dot(onehot, table[1]).astype(BF), col, coeff_row
+
+    def times(high, low, other_side, cb):
+        both = dot(jnp.concatenate([high, low], axis=0), other_side, 1, cb)
+        return both[:64] + both[64:]
+
+    def contribution(fi, high, low, col_b):
         parts = []
         for s in range(SLABS):
-            xs = xv[:, (fi * SLABS + s) * 256 : (fi * SLABS + s + 1) * 256]
-            parts.append(
-                dot(cs_high[64 * s : 64 * s + 64], xs, 1, 1)
-                + dot(cs_low[64 * s : 64 * s + 64], xs, 1, 1)
-            )
-        value = dot3(split(jnp.concatenate(parts, axis=0)), gc)
-        packed = pack(fold(value, col_b))
-        upart[fi] = packed
-        usend[fi] = packed.astype(BF)
-
-    u_copies = [
-        remote(
-            usend.at[lax.rem(f + o, NF)], urecv.at[o - 1], u_s.at[o - 1], u_r.at[o - 1], line_peer(o)
-        )
-        for o in range(1, NF)
-    ]
-    wait_g(1)
-    send_g(1)
-    send_x(2)
-
-    own = pl.multiple_of(f * 256, 256)
+            cols = pl.ds(pl.multiple_of(fi * 1024 + s * 256, 256), 256)
+            at = slice(64 * s, 64 * s + 64)
+            parts.append(times(high[at], low[at], xv[:, cols], 1))
+        return pack(fold(dot3(split(jnp.concatenate(parts, axis=0)), gc), col_b))
+
+    own_high, own_low, own_col, own_row = chosen_rows(f)
+    csh[...] = own_high
+    csl[...] = own_low
+    col_b = jnp.broadcast_to(own_col, (256, 128))
+    jrow[...] = col_b
+    trow[...] = jnp.broadcast_to(own_row + 64.0 * jnp.floor(own_col * 0.5), (256, 128))
     loads[2].wait()
     parts = []
     for s in range(SLABS):
-        high = csh[pl.ds(own + 64 * s, 64), :]
-        low = csl[pl.ds(own + 64 * s, 64), :]
-        ms = mv[256 * s : 256 * s + 256, :]
-        parts.append(dot(high, ms) + dot(low, ms))
-    col_b = jrow[pl.ds(own, 256), :]
-    from_momentum = fold(lanes_transform(jnp.concatenate(parts, axis=0), table, 1), col_b)
-    packed = upart[f] + 0.9 * pack(from_momentum)
+        at = slice(64 * s, 64 * s + 64)
+        parts.append(times(own_high[at], own_low[at], mv[256 * s : 256 * s + 256, :], 0))
+    upart[...] = 0.9 * pack(fold(lanes_transform(jnp.concatenate(parts, axis=0), table, 1), col_b))
+    loads[0].wait()
+    u_copies = []
+    for o in range(1, NF):
+        pk_copies[NF - o - 1].wait_recv()
+        fi = lax.rem(f + o, NF)
+        high, low, col, _ = chosen_rows(fi)
+        usend[o - 1] = contribution(fi, high, low, jnp.broadcast_to(col, (256, 128))).astype(BF)
+        u_copies.append(
+            remote(usend.at[o - 1], urecv.at[o - 1], u_s.at[o - 1], u_r.at[o - 1], line_peer(o))
+        )
+    wait_g(1)
+    send_g(1)
+    send_x([1])
+    col_b = jrow[...]
+    packed = upart[...] + contribution(f, csh[...], csl[...], col_b)
     for copy in u_copies:
         copy.wait_recv()
     for o in range(3):
         packed = packed + urecv[o].astype(F32)
     packed = jnp.concatenate([packed, pltpu.roll(packed, 64, 1)], axis=0)
     col_odd = col_b - 2.0 * jnp.floor(col_b * 0.5)
-    tile = jnp.where(lane < 64, packed, jnp.where(lane < 96, trow[pl.ds(own, 256), :], col_odd))
+    tile = jnp.where(lane < 64, packed, jnp.where(lane < 96, trow[...], col_odd))
     sent[...] = tile.astype(BF)
 
     a_copies = []
@@ -344,9 +345,10 @@
         remote(zb.at[zh], zb.at[zh], z_s.at[o - 1], z_r.at[o - 1], hi_peer(o))
         for o in range(1, NZ)
     ]
+    send_x([2])
     wait_g(2)
     send_g(2)
-    send_x(5)
+    send_x(range(3, PIECES))
     for copy in z_copies:
         copy.wait_recv()
     total = zb[0].astype(F32) + zb[1].astype(F32) + zb[2].astype(F32)
@@ -364,21 +366,30 @@
     ]
     lane512 = (iota((64, 512), 1) >> 6).astype(F32)
 
-    def slab(s):
-        for piece in (2 * s, 2 * s + 1):
+    m_out = []
+
+    def slab(first, count):
+        for piece in range(first, first + count):
             for copy in x_copies[piece]:
                 copy.wait_recv()
-        cols = pl.ds(pl.multiple_of(f * 1024 + s * 256, 256), 256)
-        moment = 0.9 * mv[256 * s : 256 * s + 256, :].astype(F32)
+        size = 128 * count
+        at = slice(128 * first, 128 * first + size)
+        picked = slice(32 * first, 32 * first + 32 * count)
+        part = slice(128 * (first % 2), 128 * (first % 2) + size)
+        cols = pl.ds(pl.multiple_of(f * 1024 + 128 * first, 128), size)
+        moment = 0.9 * mv[at, :].astype(F32)
         moment = moment + dot(xv[:, cols], g_all[f], 0, 0)
         for o in range(1, NF):
             source = lax.rem(f + NF - o, NF)
-            moment = moment + dot(xr[o - 1, :, 256 * s : 256 * s + 256], g_all[source], 0, 0)
-        cs = (csh[pl.ds(own + 64 * s, 64), :], csl[pl.ds(own + 64 * s, 64), :])
+            moment = moment + dot(xr[o - 1, :, at], g_all[source], 0, 0)
+        cs = (csh[picked, part], csl[picked, part])
         coeff = lanes_transform(dot3(cs, split(moment)), table, 1)
-        coeff = jnp.where(lane512 == jrow[pl.ds(own + 64 * s, 64), :1], coeff, 0.0)
+        coeff = jnp.where(lane512[: 32 * count] == jrow[picked, :1], coeff, 0.0)
         chosen = dot3(cs, split(lanes_transform(coeff, table, 0)), 0, 0)
-        out_m[256 * s : 256 * s + 256, :] = (moment - chosen).astype(BF)
+        mout[at, :] = (moment - chosen).astype(BF)
+        copy = pltpu.make_async_copy(mout.at[at, :], out_m.at[at, :], lsem.at[5 + len(m_out)])
+        copy.start()
+        m_out.append(copy)
 
     for copy in y_copies:
         copy.wait_recv()
@@ -389,18 +400,20 @@
     ]
     c_copies = [remote(fin.at[band, :], fin.at[band, :], c_s.at[0], c_r.at[0], other)]
     wait_g(3)
-    slab(0)
+    slab(0, 2)
     for o in range(1, 4):
         w_copies[o - 1].wait_recv()
         there = pl.ds(pl.multiple_of(lax.rem(m + NX - 2 * o, NX) * 128, 128), 128)
         c_copies.append(remote(fin.at[there, :], fin.at[there, :], c_s.at[o], c_r.at[o], other))
-    slab(1)
+    slab(2, 2)
+    slab(4, 2)
     for copy in c_copies:
         copy.wait_recv()
-    out_u[...] = fin[...]
-
-    slab(2)
-    slab(3)
+    u_out = pltpu.make_async_copy(fin, out_u, lsem.at[0])
+    u_out.start()
+    slab(6, 1)
+    slab(7, 1)
+
     for copy in sends:
         copy.wait_send()
     for hop in range(3):
@@ -410,6 +423,10 @@
             @pl.when(onward)
             def _():
                 copy.wait_send()
+
+    u_out.wait()
+    for copy in m_out:
+        copy.wait()
 
 
 def body(activations, output_grads, momentum, chosen_blocks):
@@ -425,12 +442,12 @@
         pltpu.VMEM((3, 256, 1024), BF),
         pltpu.VMEM((8, 16), jnp.int32),
         pltpu.VMEM((4, 8, 128), F32),
-        pltpu.VMEM((1024, 256), BF),
-        pltpu.VMEM((1024, 256), BF),
-        pltpu.VMEM((1024, 128), F32),
-        pltpu.VMEM((1024, 128), F32),
-        pltpu.VMEM((4, 128, 128), F32),
-        pltpu.VMEM((4, 128, 128), BF),
+        pltpu.VMEM((256, 256), BF),
+        pltpu.VMEM((256, 256), BF),
+        pltpu.VMEM((256, 128), F32),
+        pltpu.VMEM((256, 128), F32),
+        pltpu.VMEM((128, 128), F32),
+        pltpu.VMEM((3, 128, 128), BF),
         pltpu.VMEM((3, 128, 128), BF),
         pltpu.VMEM((256, 128), BF),
         pltpu.VMEM((8, 32, 128), BF),
@@ -438,8 +455,9 @@
         pltpu.VMEM((7, 64, 128), BF),
         pltpu.VMEM((3, 64, 128), BF),
         pltpu.VMEM((1024, 512), BF),
+        pltpu.VMEM((1024, 512), BF),
         pltpu.SemaphoreType.REGULAR,
-        dma((5,)),
+        dma((10,)),
         dma((3,)), dma((3,)), dma((24,)), dma((24,)), dma((6,)), dma((6,)),
         dma((3,)), dma((3,)), dma((7,)), dma((7,)), dma((7,)), dma((7,)),
         dma((2,)), dma((2,)), dma((7,)), dma((7,)), dma((3,)), dma((3,)),
@@ -452,7 +470,7 @@
             jax.ShapeDtypeStruct((1024, 512), BF),
         ),
         in_specs=[anywhere] * 5,
-        out_specs=(pl.BlockSpec(memory_space=pltpu.VMEM),) * 2,
+        out_specs=(anywhere, anywhere),
         scratch_shapes=scratch,
         compiler_params=pltpu.CompilerParams(
             collective_id=0, has_side_effects=True, vmem_limit_bytes=62 * 1024 * 1024

time: 84.8 us -> 81.5 us (0.961); the launches traced: 83.2 us -> 81.3 us
  Pallas kernels: 78.6 us -> 76.8 us
    pallas_call x1, Pallas kernels: 78.6 us -> 76.8 us  [body(): pl.pallas_call(kernel, out_shape=(jax.ShapeDtypeStruct((1024, 512), BF),...]
where the time goes in v4:
time: 81.5 us; the launch traced here: 81.3 us
  Pallas kernels  76.8 us (94%)
  other arithmetic  2.92 us (4%)
  local copies, waits for them, and re-layouts  0.97 us (1%)
    pallas_call x1, Pallas kernels, body(): pl.pallas_call(kernel, out_shape=(jax.ShapeDtypeStruct((1024, 512), BF),...  76.8 us
    convert_element_type x1, other arithmetic, body(): return (moment_next[None], update.astype(F32))  2.92 us

profile of v4, /device:TPU:1, one launch (start us, length us, event | category | flops | bytes accessed | tf_op | source)
XLA Modules:
  0.0 81.3 jit_solution(2227831833732025501)
XLA Ops:
  0.6 76.8 %step.1 = (bf16[1024,512]{1,0:T(8,128)(2,1)}, bf16[1024,512]{1,0:T(8,128)(2,1)}) custom-call(bf16[256,4096]{1,0:T(8,128)(2,1)} %x_hbm.1, bf16[256,512]{1,0:T(8,128)(2,1)} %g_hbm.1, bf16[1,1024,512]{2,1,0:T(8,128)(2,1)} %mom_hbm.1, s32[8,16]{1,0:T(8,128)} %bitcast.5, bf16[4,256,256]{2,1,0:T(8,128)(2,1)} %constant.2.clone.tab_hbm), custom_call_target="tpu_custom_call" | custom-call | tf_op jit(solution)/shard_map/step/pallas_call | solution.py:466
  77.4 0.0 copy-start
  77.4 2.9 %convert_element_type.3 = f32[1024,512]{1,0:T(8,128)} convert(bf16[1024,512]{1,0:T(8,128)(2,1)} %get-tuple-element.5) | non-fusion elementwise | flops 524288 | bytes 3145728 | tf_op jit(solution)/shard_map/convert_element_type | solution.py:483
  80.4 0.0 copy-done
  80.4 1.0 %copy.8 = bf16[1,1024,512]{2,1,0:T(8,128)(2,1)} copy(bf16[1,1024,512]{2,1,0:T(8,128)(2,1)S(1)} %bitcast.4) | data formatting | bytes 2097152
Async XLA Ops:
  77.4 2.9 %copy-start = (bf16[1024,512]{1,0:T(8,128)(2,1)S(1)}, bf16[1024,512]{1,0:T(8,128)(2,1)}, u32[]{:S(2)}) copy-start(bf16[1024,512]{1,0:T(8,128)(2,1)} %get-tuple-element.4) | copy-start | bytes 3145732

commit v5 on v4

--- a/solution.py
+++ b/solution.py
@@ -168,7 +168,7 @@
             for step in range(NF - 1) if offsets is None else offsets:
                 o = step
                 if offsets is None:
-                    target = step + 1 - lax.div(f + NF - 1 - step, NF)
+                    target = NF - 1 - step - lax.div(f + 1 + step, NF)
                     o = lax.rem(target - f + NF, NF)
                 peer = lax.rem(f + o, NF)
                 cols = pl.ds(pl.multiple_of(peer * 1024 + piece * 128, 128), 128)
@@ -286,6 +286,7 @@
     wait_g(1)
     send_g(1)
     send_x([1])
+    send_x([2], (2,))
     col_b = jrow[...]
     packed = upart[...] + contribution(f, csh[...], csl[...], col_b)
     for copy in u_copies:
@@ -345,7 +346,7 @@
         remote(zb.at[zh], zb.at[zh], z_s.at[o - 1], z_r.at[o - 1], hi_peer(o))
         for o in range(1, NZ)
     ]
-    send_x([2])
+    send_x([2], (3, 1))
     wait_g(2)
     send_g(2)
     send_x(range(3, PIECES))

time: 81.5 us -> 83 us (1.018)
  Pallas kernels: 76.8 us -> 78.3 us
    pallas_call x1, Pallas kernels: 76.8 us -> 78.3 us  [body(): pl.pallas_call(kernel, out_shape=(jax.ShapeDtypeStruct((1024, 512), BF),...]
where the time goes in v5:
time: 83 us; the launch traced here: 82.8 us
  Pallas kernels  78.3 us (94%)
  other arithmetic  2.92 us (4%)
  local copies, waits for them, and re-layouts  0.97 us (1%)
    pallas_call x1, Pallas kernels, body(): pl.pallas_call(kernel, out_shape=(jax.ShapeDtypeStruct((1024, 512), BF),...  78.3 us
    convert_element_type x1, other arithmetic, body(): return (moment_next[None], update.astype(F32))  2.92 us

profile of v5, /device:TPU:1, one launch (start us, length us, event | category | flops | bytes accessed | tf_op | source)
XLA Modules:
  0.0 82.8 jit_solution(10923721118324254670)
XLA Ops:
  0.6 78.3 %step.1 = (bf16[1024,512]{1,0:T(8,128)(2,1)}, bf16[1024,512]{1,0:T(8,128)(2,1)}) custom-call(bf16[256,4096]{1,0:T(8,128)(2,1)} %x_hbm.1, bf16[256,512]{1,0:T(8,128)(2,1)} %g_hbm.1, bf16[1,1024,512]{2,1,0:T(8,128)(2,1)} %mom_hbm.1, s32[8,16]{1,0:T(8,128)} %bitcast.5, bf16[4,256,256]{2,1,0:T(8,128)(2,1)} %constant.2.clone.tab_hbm), custom_call_target="tpu_custom_call" | custom-call | tf_op jit(solution)/shard_map/step/pallas_call | solution.py:467
  78.9 0.0 copy-start
  78.9 2.9 %convert_element_type.3 = f32[1024,512]{1,0:T(8,128)} convert(bf16[1024,512]{1,0:T(8,128)(2,1)} %get-tuple-element.5) | non-fusion elementwise | flops 524288 | bytes 3145728 | tf_op jit(solution)/shard_map/convert_element_type | solution.py:484
  81.8 0.0 copy-done
  81.8 1.0 %copy.8 = bf16[1,1024,512]{2,1,0:T(8,128)(2,1)} copy(bf16[1,1024,512]{2,1,0:T(8,128)(2,1)S(1)} %bitcast.4) | data formatting | bytes 2097152
Async XLA Ops:
  78.9 2.9 %copy-start = (bf16[1024,512]{1,0:T(8,128)(2,1)S(1)}, bf16[1024,512]{1,0:T(8,128)(2,1)}, u32[]{:S(2)}) copy-start(bf16[1024,512]{1,0:T(8,128)(2,1)} %get-tuple-element.4) | copy-start | bytes 3145732
